TPU v7x, 32 devices: a whole 2x2x4 slice. The times are simulated.
32 devices in a mesh: pipe: 4 (over z), dp: 2 (over x), tensor: 4 (over y, core).
Axes of the slice: x: 2, y: 2, z: 4, core: 2. Of those that a mesh axis runs over, the one named last changes fastest.
Arguments:
- acts: bfloat16 [4, 4, 128, 8192], P('pipe', None, 'dp', 'tensor'), may hold values from -6 to 6
- w_in: bfloat16 [4, 8192, 512], P('pipe', 'tensor', 'dp'), may hold values from -0.0625 to 0.0625
- w_out: bfloat16 [4, 512, 8192], P('pipe', 'dp', 'tensor'), may hold values from -0.25 to 0.25
- top_grad: bfloat16 [4, 128, 8192], P(None, 'dp', 'tensor'), may hold values from -6 to 6
Outputs:
- grad_input: bfloat16 [4, 4, 128, 8192], P('pipe', None, 'dp', 'tensor')
- grad_w_in: bfloat16 [4, 8192, 512], P('pipe', 'tensor', 'dp')
- grad_w_out: bfloat16 [4, 512, 8192], P('pipe', 'dp', 'tensor')
All inputs are finite; a program needn't handle non-finite values.
Results may differ from a plain program's by a relative error of at most 0.013.
Values may be sent and summed in bfloat16 or wider, within the bound.
A program may use at most 64 MiB of HBM per device.

v0:
```python
import jax
import jax.numpy as jnp
from jax import lax
from jax.sharding import PartitionSpec as P


def shifted(shard, axis, by):
    devices = lax.axis_size(axis)
    pairs = [(i, i + by) for i in range(devices) if 0 <= i + by < devices]
    return lax.ppermute(shard, axis, pairs)


def silu_slope(value):
    sig = jax.nn.sigmoid(value)
    return sig * (1.0 + value * (1.0 - sig))


def put_slot(store, piece, slot, active):
    updated = lax.dynamic_update_index_in_dim(store, piece, slot, 0)
    return jnp.where(active, updated, store)


def shards(acts, w_in, w_out, top_grad):
    pipes = lax.axis_size("pipe")
    section = lax.axis_index("pipe")
    micro = acts.shape[1]
    rows = acts.shape[2]
    width = acts.shape[3]
    saved = acts[0]
    w_in_full, w_out_full = (
        lax.all_gather(w_in[0], "dp", axis=1, tiled=True),
        lax.all_gather(w_out[0], "dp", axis=0, tiled=True),
    )
    inner = w_in_full.shape[1]
    contract = (((1,), (1,)), ((), ()))
    incoming = jnp.zeros((rows, width), jnp.bfloat16)
    dpre_store = jnp.zeros((micro, rows, inner), jnp.bfloat16)
    act_store = jnp.zeros((micro, rows, inner), jnp.bfloat16)
    grad_store = jnp.zeros((micro, rows, width), jnp.bfloat16)
    back_store = jnp.zeros((micro, rows, width), jnp.bfloat16)
    total_steps = micro + pipes - 1
    for step in range(total_steps):
        index = step - (pipes - 1 - section)
        active = jnp.logical_and(index >= 0, index < micro)
        slot = jnp.clip(index, 0, micro - 1)
        top_piece = lax.dynamic_index_in_dim(top_grad, slot, 0, keepdims=False)
        grad_now = jnp.where(section == pipes - 1, top_piece, incoming)
        x_now = lax.dynamic_index_in_dim(saved, slot, 0, keepdims=False)
        pre_part = jnp.dot(x_now, w_in_full, preferred_element_type=jnp.float32)
        pre_now = lax.psum(pre_part, "tensor")
        hidden_part = lax.dot_general(
            grad_now, w_out_full, contract, preferred_element_type=jnp.float32
        )
        hidden = lax.psum(hidden_part, "tensor")
        dpre = (hidden * silu_slope(pre_now)).astype(jnp.bfloat16)
        branch = lax.dot_general(dpre, w_in_full, contract, preferred_element_type=jnp.float32)
        back = (grad_now.astype(jnp.float32) + branch).astype(jnp.bfloat16)
        dpre_store = put_slot(dpre_store, dpre, slot, active)
        act_store = put_slot(act_store, jax.nn.silu(pre_now).astype(jnp.bfloat16), slot, active)
        grad_store = put_slot(grad_store, grad_now, slot, active)
        back_store = put_slot(back_store, back, slot, active)
        if step + 1 < total_steps:
            incoming = shifted(back, "pipe", -1)
    token_dims = (((0,), (0,)), ((), ()))
    flat_x = saved.reshape(micro * rows, width)
    part_in = lax.dot_general(
        flat_x,
        dpre_store.reshape(micro * rows, inner),
        token_dims,
        preferred_element_type=jnp.float32,
    )
    part_out = lax.dot_general(
        act_store.reshape(micro * rows, inner),
        grad_store.reshape(micro * rows, width),
        token_dims,
        preferred_element_type=jnp.float32,
    )
    summed_in, summed_out = (
        lax.psum_scatter(
            part_in.astype(jnp.bfloat16), "dp", scatter_dimension=1, tiled=True
        ).astype(jnp.float32),
        lax.psum_scatter(
            part_out.astype(jnp.bfloat16), "dp", scatter_dimension=0, tiled=True
        ).astype(jnp.float32),
    )
    return (
        back_store[None],
        summed_in.astype(jnp.bfloat16)[None],
        summed_out.astype(jnp.bfloat16)[None],
    )


def solution(mesh):
    placed = (
        P("pipe", None, "dp", "tensor"),
        P("pipe", "tensor", "dp"),
        P("pipe", "dp", "tensor"),
        P(None, "dp", "tensor"),
    )
    return jax.shard_map(
        shards,
        mesh=mesh,
        in_specs=placed,
        out_specs=(
            P("pipe", None, "dp", "tensor"),
            P("pipe", "tensor", "dp"),
            P("pipe", "dp", "tensor"),
        ),
        check_vma=False,
    )
```

profile of v0, /device:TPU:0, one launch (start us, length us, event | category | flops | bytes accessed | tf_op | source)
XLA Modules:
  0.0 486.9 jit_solution(4687135771134606875)
XLA Ops:
  8.7 36.6 %all-gather.7.cloned.1.call-done = bf16[1,2048,512]{2,1,0:T(8,128)(2,1)} async-done(((bf16[1,2048,256]{2,1,0:T(8,128)(2,1)}), bf16[1,2048,512]{2,1,0:T(8,128)(2,1)}) %all-gather.7.cloned.1.call-update) | async-done | bytes 2097168 | tf_op jit(solution)/shard_map/all_gather | solution.py:31
  45.4 2.7 fusion.27
  48.1 32.0 %all-gather.5.cloned.1.call-done = bf16[1,512,2048]{2,1,0:T(8,128)(2,1)} async-done(((bf16[1,256,2048]{2,1,0:T(8,128)(2,1)}), bf16[1,512,2048]{2,1,0:T(8,128)(2,1)}) %all-gather.5.cloned.1.call-update) | async-done | bytes 2097168 | tf_op jit(solution)/shard_map/all_gather | solution.py:32
  80.1 3.1 fusion.41
  86.0 29.4 %all-reduce.27.cloned.1.call-done = (f32[64,512]{1,0:T(8,128)}, f32[64,512]{1,0:T(8,128)}) async-done(((f32[64,512]{1,0:T(8,128)}, f32[64,512]{1,0:T(8,128)}), (f32[64,512]{1,0:T(8,128)}, f32[64,512]{1,0:T(8,128)})) %all-reduce.27.cloned.1.call-update) | async-done | bytes 262160 | tf_op jit(solution)/shard_map/psum | solution.py:54
  117.6 2.4 bitcast_dynamic-update-slice_fusion
  122.6 6.3 %collective-permute-done = bf16[64,2048]{1,0:T(8,128)(2,1)S(1)} collective-permute-done((bf16[64,2048]{1,0:T(8,128)(2,1)S(1)}, bf16[64,2048]{1,0:T(8,128)(2,1)S(1)}, u32[]{:S(2)}, u32[]{:S(2)}) %collective-permute-start) | collective-permute-done | bytes 262176 | tf_op jit(solution)/shard_map/ppermute | solution.py:10
  128.8 1.8 fusion.52
  134.3 30.6 %all-reduce.25.cloned.1.call-done = (f32[64,512]{1,0:T(8,128)}, f32[64,512]{1,0:T(8,128)}) async-done(((f32[64,512]{1,0:T(8,128)}, f32[64,512]{1,0:T(8,128)}), (f32[64,512]{1,0:T(8,128)}, f32[64,512]{1,0:T(8,128)})) %all-reduce.25.cloned.1.call-update) | async-done | bytes 262160 | tf_op jit(solution)/shard_map/psum | solution.py:54
  166.5 2.5 fusion.62
  171.6 6.3 %collective-permute-done.1 = bf16[64,2048]{1,0:T(8,128)(2,1)S(1)} collective-permute-done((bf16[64,2048]{1,0:T(8,128)(2,1)S(1)}, bf16[64,2048]{1,0:T(8,128)(2,1)S(1)}, u32[]{:S(2)}, u32[]{:S(2)}) %collective-permute-start.1) | collective-permute-done | bytes 262176 | tf_op jit(solution)/shard_map/ppermute | solution.py:10
  177.8 1.8 fusion.51
  181.9 32.0 %all-reduce.23.cloned.1.call-done = (f32[64,512]{1,0:T(8,128)}, f32[64,512]{1,0:T(8,128)}) async-done(((f32[64,512]{1,0:T(8,128)}, f32[64,512]{1,0:T(8,128)}), (f32[64,512]{1,0:T(8,128)}, f32[64,512]{1,0:T(8,128)})) %all-reduce.23.cloned.1.call-update) | async-done | bytes 262160 | tf_op jit(solution)/shard_map/psum | solution.py:54
  215.5 2.5 fusion.60
  220.5 6.3 %collective-permute-done.2 = bf16[64,2048]{1,0:T(8,128)(2,1)S(1)} collective-permute-done((bf16[64,2048]{1,0:T(8,128)(2,1)S(1)}, bf16[64,2048]{1,0:T(8,128)(2,1)S(1)}, u32[]{:S(2)}, u32[]{:S(2)}) %collective-permute-start.2) | collective-permute-done | bytes 262176 | tf_op jit(solution)/shard_map/ppermute | solution.py:10
  230.9 32.0 %all-reduce.21.cloned.1.call-done = (f32[64,512]{1,0:T(8,128)}, f32[64,512]{1,0:T(8,128)}) async-done(((f32[64,512]{1,0:T(8,128)}, f32[64,512]{1,0:T(8,128)}), (f32[64,512]{1,0:T(8,128)}, f32[64,512]{1,0:T(8,128)})) %all-reduce.21.cloned.1.call-update) | async-done | bytes 262160 | tf_op jit(solution)/shard_map/psum | solution.py:54
  264.5 2.5 fusion.58
  269.6 6.3 %collective-permute-done.3 = bf16[64,2048]{1,0:T(8,128)(2,1)S(1)} collective-permute-done((bf16[64,2048]{1,0:T(8,128)(2,1)S(1)}, bf16[64,2048]{1,0:T(8,128)(2,1)S(1)}, u32[]{:S(2)}, u32[]{:S(2)}) %collective-permute-start.3) | collective-permute-done | bytes 262176 | tf_op jit(solution)/shard_map/ppermute | solution.py:10
  279.9 32.0 %all-reduce.19.cloned.1.call-done = (f32[64,512]{1,0:T(8,128)}, f32[64,512]{1,0:T(8,128)}) async-done(((f32[64,512]{1,0:T(8,128)}, f32[64,512]{1,0:T(8,128)}), (f32[64,512]{1,0:T(8,128)}, f32[64,512]{1,0:T(8,128)})) %all-reduce.19.cloned.1.call-update) | async-done | bytes 262160 | tf_op jit(solution)/shard_map/psum | solution.py:54
  313.5 2.5 fusion.56
  318.5 6.3 %collective-permute-done.4 = bf16[64,2048]{1,0:T(8,128)(2,1)S(1)} collective-permute-done((bf16[64,2048]{1,0:T(8,128)(2,1)S(1)}, bf16[64,2048]{1,0:T(8,128)(2,1)S(1)}, u32[]{:S(2)}, u32[]{:S(2)}) %collective-permute-start.4) | collective-permute-done | bytes 262176 | tf_op jit(solution)/shard_map/ppermute | solution.py:10
  328.9 32.0 %all-reduce.17.cloned.1.call-done = (f32[64,512]{1,0:T(8,128)}, f32[64,512]{1,0:T(8,128)}) async-done(((f32[64,512]{1,0:T(8,128)}, f32[64,512]{1,0:T(8,128)}), (f32[64,512]{1,0:T(8,128)}, f32[64,512]{1,0:T(8,128)})) %all-reduce.17.cloned.1.call-update) | async-done | bytes 262160 | tf_op jit(solution)/shard_map/psum | solution.py:54
  362.5 2.5 fusion.54
  367.5 6.3 %collective-permute-done.5 = bf16[64,2048]{1,0:T(8,128)(2,1)S(1)} collective-permute-done((bf16[64,2048]{1,0:T(8,128)(2,1)S(1)}, bf16[64,2048]{1,0:T(8,128)(2,1)S(1)}, u32[]{:S(2)}, u32[]{:S(2)}) %collective-permute-start.5) | collective-permute-done | bytes 262176 | tf_op jit(solution)/shard_map/ppermute | solution.py:10
  377.8 32.0 %all-reduce.15.cloned.1.call-done = (f32[64,512]{1,0:T(8,128)}, f32[64,512]{1,0:T(8,128)}) async-done(((f32[64,512]{1,0:T(8,128)}, f32[64,512]{1,0:T(8,128)}), (f32[64,512]{1,0:T(8,128)}, f32[64,512]{1,0:T(8,128)})) %all-reduce.15.cloned.1.call-update) | async-done | bytes 262160 | tf_op jit(solution)/shard_map/psum | solution.py:54
  411.5 2.1 fusion
  413.7 3.4 bitcast_convert_fusion
  417.1 2.3 copy.49
  419.4 2.5 fusion.46
  421.9 23.7 %reduce-scatter.3.cloned.1.call-done = bf16[2048,256]{0,1:T(8,128)(2,1)} async-done(((bf16[2048,512]{0,1:T(8,128)(2,1)}), bf16[2048,256]{0,1:T(8,128)(2,1)}) %reduce-scatter.3.cloned.1.call-update) | async-done | bytes 1048592 | tf_op jit(solution)/shard_map/reduce_scatter | solution.py:79
  445.6 2.3 copy.7
  447.9 32.5 %reduce-scatter.5.cloned.1.call-done = bf16[256,2048]{1,0:T(8,128)(2,1)} async-done(((bf16[512,2048]{1,0:T(8,128)(2,1)}), bf16[256,2048]{1,0:T(8,128)(2,1)}) %reduce-scatter.5.cloned.1.call-update) | async-done | bytes 1048592 | tf_op jit(solution)/shard_map/reduce_scatter | solution.py:82
  (89 shorter events, 53.6 us)
Async XLA Ops:
  7.2 38.2 %copy-start = (bf16[1,4,64,2048]{3,2,1,0:T(8,128)(2,1)S(1)}, bf16[1,4,64,2048]{3,2,1,0:T(8,128)(2,1)}, u32[]{:S(2)}) copy-start(bf16[1,4,64,2048]{3,2,1,0:T(8,128)(2,1)} %param.4) | copy-start | bytes 3145732
  7.2 38.2 %all-gather.7.cloned.1.call-start = ((), (), s32[]{:S(2)}) async-start(), calls=%async_computation.5 | async-start | bytes 3145728 | tf_op jit(solution)/shard_map/all_gather | solution.py:31
  7.9 72.1 %all-gather.5.cloned.1.call-start = ((), (), s32[]{:S(2)}) async-start(), calls=%async_computation.4 | async-start | bytes 3145728 | tf_op jit(solution)/shard_map/all_gather | solution.py:32
  8.7 106.8 %all-reduce.27.cloned.1.call-start = ((), (), s32[]{:S(2)}) async-start(), calls=%async_computation.12 | async-start | bytes 524288 | tf_op jit(solution)/shard_map/psum | solution.py:54
  83.2 34.4 %copy-start.1 = (bf16[1,2048,512]{2,1,0:T(8,128)(2,1)S(1)}, bf16[1,2048,512]{2,1,0:T(8,128)(2,1)}, u32[]{:S(2)}) copy-start(bf16[1,2048,512]{2,1,0:T(8,128)(2,1)} %all-gather.7.cloned.1.call-done) | copy-start | bytes 6291460
  83.2 81.7 %all-reduce.25.cloned.1.call-start = ((), (), s32[]{:S(2)}) async-start(), calls=%async_computation.11 | async-start | bytes 524288 | tf_op jit(solution)/shard_map/psum | solution.py:54
  120.0 11.4 %copy-start.2 = (bf16[1,512,2048]{2,1,0:T(8,128)(2,1)S(1)}, bf16[1,512,2048]{2,1,0:T(8,128)(2,1)}, u32[]{:S(2)}) copy-start(bf16[1,512,2048]{2,1,0:T(8,128)(2,1)} %all-gather.5.cloned.1.call-done) | copy-start | bytes 6291460
  120.0 8.8 %collective-permute-start = (bf16[64,2048]{1,0:T(8,128)(2,1)S(1)}, bf16[64,2048]{1,0:T(8,128)(2,1)S(1)}, u32[]{:S(2)}, u32[]{:S(2)}) collective-permute-start(bf16[64,2048]{1,0:T(8,128)(2,1)S(1)} %get-tuple-element.63), channel_id=1, source_target_pairs={{8,0},{16,8},{24,16},{9,1},{17,9},{25,17},{10,2},{18,10},{26,18},{... | collective-permute-start | bytes 786440 | tf_op jit(solution)/shard_map/ppermute | solution.py:10
  122.6 11.0 %copy-start.15 = (f32[64,512]{1,0:T(8,128)S(1)}, f32[64,512]{1,0:T(8,128)}, u32[]{:S(2)}) copy-start(f32[64,512]{1,0:T(8,128)} %get-tuple-element.19) | copy-start | bytes 393220
  130.7 0.7 copy-start.12
  132.8 81.0 %all-reduce.23.cloned.1.call-start = ((), (), s32[]{:S(2)}) async-start(), calls=%async_computation.10 | async-start | bytes 524288 | tf_op jit(solution)/shard_map/psum | solution.py:54
  169.0 11.4 %copy-start.3 = (bf16[1,512,2048]{2,1,0:T(8,128)(2,1)S(1)}, bf16[1,512,2048]{2,1,0:T(8,128)(2,1)}, u32[]{:S(2)}) copy-start(bf16[1,512,2048]{2,1,0:T(8,128)(2,1)} %all-gather.5.cloned.1.call-done) | copy-start | bytes 6291460
  169.0 8.8 %collective-permute-start.1 = (bf16[64,2048]{1,0:T(8,128)(2,1)S(1)}, bf16[64,2048]{1,0:T(8,128)(2,1)S(1)}, u32[]{:S(2)}, u32[]{:S(2)}) collective-permute-start(bf16[64,2048]{1,0:T(8,128)(2,1)S(1)} %get-tuple-element.55), channel_id=1, source_target_pairs={{8,0},{16,8},{24,16},{9,1},{17,9},{25,17},{10,2},{18,10},{26,18},{... | collective-permute-start | bytes 786440 | tf_op jit(solution)/shard_map/ppermute | solution.py:10
  179.7 0.7 copy-start.11
  181.8 81.0 %all-reduce.21.cloned.1.call-start = ((), (), s32[]{:S(2)}) async-start(), calls=%async_computation.9 | async-start | bytes 524288 | tf_op jit(solution)/shard_map/psum | solution.py:54
  218.0 11.4 %copy-start.4 = (bf16[1,512,2048]{2,1,0:T(8,128)(2,1)S(1)}, bf16[1,512,2048]{2,1,0:T(8,128)(2,1)}, u32[]{:S(2)}) copy-start(bf16[1,512,2048]{2,1,0:T(8,128)(2,1)} %all-gather.5.cloned.1.call-done) | copy-start | bytes 6291460
  218.0 8.8 %collective-permute-start.2 = (bf16[64,2048]{1,0:T(8,128)(2,1)S(1)}, bf16[64,2048]{1,0:T(8,128)(2,1)S(1)}, u32[]{:S(2)}, u32[]{:S(2)}) collective-permute-start(bf16[64,2048]{1,0:T(8,128)(2,1)S(1)} %get-tuple-element.53), channel_id=1, source_target_pairs={{8,0},{16,8},{24,16},{9,1},{17,9},{25,17},{10,2},{18,10},{26,18},{... | collective-permute-start | bytes 786440 | tf_op jit(solution)/shard_map/ppermute | solution.py:10
  228.7 0.7 copy-start.10
  230.8 81.0 %all-reduce.19.cloned.1.call-start = ((), (), s32[]{:S(2)}) async-start(), calls=%async_computation.8 | async-start | bytes 524288 | tf_op jit(solution)/shard_map/psum | solution.py:54
  267.0 11.4 %copy-start.5 = (bf16[1,512,2048]{2,1,0:T(8,128)(2,1)S(1)}, bf16[1,512,2048]{2,1,0:T(8,128)(2,1)}, u32[]{:S(2)}) copy-start(bf16[1,512,2048]{2,1,0:T(8,128)(2,1)} %all-gather.5.cloned.1.call-done) | copy-start | bytes 6291460
  267.0 8.8 %collective-permute-start.3 = (bf16[64,2048]{1,0:T(8,128)(2,1)S(1)}, bf16[64,2048]{1,0:T(8,128)(2,1)S(1)}, u32[]{:S(2)}, u32[]{:S(2)}) collective-permute-start(bf16[64,2048]{1,0:T(8,128)(2,1)S(1)} %get-tuple-element.51), channel_id=1, source_target_pairs={{8,0},{16,8},{24,16},{9,1},{17,9},{25,17},{10,2},{18,10},{26,18},{... | collective-permute-start | bytes 786440 | tf_op jit(solution)/shard_map/ppermute | solution.py:10
  277.7 0.7 copy-start.9
  279.8 81.0 %all-reduce.17.cloned.1.call-start = ((), (), s32[]{:S(2)}) async-start(), calls=%async_computation.7 | async-start | bytes 524288 | tf_op jit(solution)/shard_map/psum | solution.py:54
  316.0 11.4 %copy-start.6 = (bf16[1,512,2048]{2,1,0:T(8,128)(2,1)S(1)}, bf16[1,512,2048]{2,1,0:T(8,128)(2,1)}, u32[]{:S(2)}) copy-start(bf16[1,512,2048]{2,1,0:T(8,128)(2,1)} %all-gather.5.cloned.1.call-done) | copy-start | bytes 6291460
  316.0 8.8 %collective-permute-start.4 = (bf16[64,2048]{1,0:T(8,128)(2,1)S(1)}, bf16[64,2048]{1,0:T(8,128)(2,1)S(1)}, u32[]{:S(2)}, u32[]{:S(2)}) collective-permute-start(bf16[64,2048]{1,0:T(8,128)(2,1)S(1)} %get-tuple-element.49), channel_id=1, source_target_pairs={{8,0},{16,8},{24,16},{9,1},{17,9},{25,17},{10,2},{18,10},{26,18},{... | collective-permute-start | bytes 786440 | tf_op jit(solution)/shard_map/ppermute | solution.py:10
  326.7 0.7 copy-start.8
  328.8 81.0 %all-reduce.15.cloned.1.call-start = ((), (), s32[]{:S(2)}) async-start(), calls=%async_computation.6 | async-start | bytes 524288 | tf_op jit(solution)/shard_map/psum | solution.py:54
  365.0 11.4 %copy-start.7 = (bf16[1,512,2048]{2,1,0:T(8,128)(2,1)S(1)}, bf16[1,512,2048]{2,1,0:T(8,128)(2,1)}, u32[]{:S(2)}) copy-start(bf16[1,512,2048]{2,1,0:T(8,128)(2,1)} %all-gather.5.cloned.1.call-done) | copy-start | bytes 6291460
  365.0 8.8 %collective-permute-start.5 = (bf16[64,2048]{1,0:T(8,128)(2,1)S(1)}, bf16[64,2048]{1,0:T(8,128)(2,1)S(1)}, u32[]{:S(2)}, u32[]{:S(2)}) collective-permute-start(bf16[64,2048]{1,0:T(8,128)(2,1)S(1)} %get-tuple-element.47), channel_id=1, source_target_pairs={{8,0},{16,8},{24,16},{9,1},{17,9},{25,17},{10,2},{18,10},{26,18},{... | collective-permute-start | bytes 786440 | tf_op jit(solution)/shard_map/ppermute | solution.py:10
  377.8 67.8 %reduce-scatter.3.cloned.1.call-start = ((), (), s32[]{:S(2)}) async-start(), calls=%async_computation.2 | async-start | bytes 3145728 | tf_op jit(solution)/shard_map/reduce_scatter | solution.py:79
  413.6 66.8 %reduce-scatter.5.cloned.1.call-start = ((), (), s32[]{:S(2)}) async-start(), calls=%async_computation.3 | async-start | bytes 3145728 | tf_op jit(solution)/shard_map/reduce_scatter | solution.py:82
  417.1 2.4 copy-start.14
  (1 other events, 0.7 us)
Sparse Core Ops, SparseCore 0:
  9.5 35.7 all-gather.6
  46.9 33.1 all-gather.4
  83.3 32.0 all-reduce.26
  132.9 31.8 all-reduce.24
  181.9 31.8 all-reduce.22
  230.9 31.8 all-reduce.20
  279.9 31.8 all-reduce.18
  328.9 31.8 all-reduce.16
  377.9 31.8 all-reduce.14
  413.7 31.8 reduce-scatter.2
  448.4 31.8 reduce-scatter.4
where the time goes:
time: 488 us; the launch traced here: 487 us
  waiting for transfers between devices  384 us (79%)
  matrix products  44 us (9%)
  other arithmetic  24.4 us (5%)
  between operations  14 us (3%)
  local copies, waits for them, and re-layouts  11.8 us (2%)
  starting transfers between devices  8.92 us (2%)
    psum x7, waiting for transfers between devices, shards(): hidden = lax.psum(hidden_part, 'tensor')  220 us
    ppermute x6, waiting for transfers between devices, shifted(): return lax.ppermute(shard, axis, pairs)  37.7 us
    all_gather x1, waiting for transfers between devices, shards(): lax.all_gather(w_in[0], 'dp', axis=1, tiled=True)  36.6 us
    reduce_scatter x1, waiting for transfers between devices, shards(): lax.psum_scatter(part_out.astype(jnp.bfloat16), 'dp', scatter_dimension=0...  32.5 us
    all_gather x1, waiting for transfers between devices, shards(): lax.all_gather(w_out[0], 'dp', axis=0, tiled=True)  32 us
    select_n x15, other arithmetic, put_slot(): return jnp.where(active, updated, store)  24.4 us
    reduce_scatter x1, waiting for transfers between devices, shards(): lax.psum_scatter(part_in.astype(jnp.bfloat16), 'dp', scatter_dimension=1,...  23.7 us
    dot_general x7, matrix products, shards(): lax.dot_general(dpre, w_in_full, contract, preferred_element_type=jnp.flo...  17.4 us
  transfers between devices with their start and end apart: 17, of which 17 were waited for; matrix products, arithmetic and copies ran while one was open for 5% of the time, Pallas kernels for 0%

commit v1 on v0

--- a/solution.py
+++ b/solution.py
@@ -2,6 +2,10 @@
 import jax.numpy as jnp
 from jax import lax
 from jax.sharding import PartitionSpec as P
+
+
+def refer_vector(inner_x):
+    return jax.lax.all_gather(inner_x, "tensor").sum(axis=0)
 
 
 def shifted(shard, axis, by):
@@ -51,7 +55,7 @@
         hidden_part = lax.dot_general(
             grad_now, w_out_full, contract, preferred_element_type=jnp.float32
         )
-        hidden = lax.psum(hidden_part, "tensor")
+        hidden = refer_vector(hidden_part)
         dpre = (hidden * silu_slope(pre_now)).astype(jnp.bfloat16)
         branch = lax.dot_general(dpre, w_in_full, contract, preferred_element_type=jnp.float32)
         back = (grad_now.astype(jnp.float32) + branch).astype(jnp.bfloat16)

time: 488 us -> 366 us (0.75)
  waiting for transfers between devices: 384 us -> 198 us
  blocking collectives: 0 us -> 50.7 us
  other arithmetic: 24.4 us -> 31.5 us
  matrix products: 44 us -> 49.3 us
    psum x7 -> x1, waiting for transfers between devices: 220 us -> 28.3 us  [shards(): pre_now = lax.psum(pre_part, 'tensor')]
    all_gather x0 -> x7, blocking collectives: none -> 50.7 us  [refer_vector(): return jax.lax.all_gather(inner_x, 'tensor').sum(axis=0)]
    ppermute x6, waiting for transfers between devices: 37.7 us -> 51.8 us  [shifted(): return lax.ppermute(shard, axis, pairs)]
    reduce_sum x0 -> x7, other arithmetic: none -> 7.62 us  [refer_vector(): return jax.lax.all_gather(inner_x, 'tensor').sum(axis=0)]
    all_gather x1, waiting for transfers between devices: 32 us -> 25 us  [shards(): lax.all_gather(w_out[0], 'dp', axis=0, tiled=True)]
    dot_general x7, matrix products: 11.6 us -> 16.5 us  [shards(): lax.dot_general(grad_now, w_out_full, contract, preferred_element_type=jn...]
    unnamed x34 -> x28, local copies, waits for them, and re-layouts: 8.85 us -> 10.4 us
  transfers between devices with their start and end apart: 17 -> 11, of which waited for: 17 -> 11; matrix products, arithmetic and copies ran while one was open for 5% -> 7% of each run, Pallas kernels for 0% -> 0%
where the time goes in v1:
time: 366 us; the launch traced here: 364 us
  waiting for transfers between devices  198 us (54%)
  blocking collectives  50.7 us (14%)
  matrix products  49.3 us (13%)
  other arithmetic  31.5 us (9%)
  between operations  14 us (4%)
  local copies, waits for them, and re-layouts  12.6 us (3%)
  starting transfers between devices  8.06 us (2%)
    ppermute x6, waiting for transfers between devices, shifted(): return lax.ppermute(shard, axis, pairs)  51.8 us
    all_gather x7, blocking collectives, refer_vector(): return jax.lax.all_gather(inner_x, 'tensor').sum(axis=0)  50.7 us
    all_gather x1, waiting for transfers between devices, shards(): lax.all_gather(w_in[0], 'dp', axis=1, tiled=True)  36.6 us
    reduce_scatter x1, waiting for transfers between devices, shards(): lax.psum_scatter(part_out.astype(jnp.bfloat16), 'dp', scatter_dimension=0...  32.4 us
    psum x1, waiting for transfers between devices, shards(): pre_now = lax.psum(pre_part, 'tensor')  28.3 us
    all_gather x1, waiting for transfers between devices, shards(): lax.all_gather(w_out[0], 'dp', axis=0, tiled=True)  25 us
    select_n x15, other arithmetic, put_slot(): return jnp.where(active, updated, store)  23.9 us
    reduce_scatter x1, waiting for transfers between devices, shards(): lax.psum_scatter(part_in.astype(jnp.bfloat16), 'dp', scatter_dimension=1,...  22.7 us
  transfers between devices with their start and end apart: 11, of which 11 were waited for; matrix products, arithmetic and copies ran while one was open for 7% of the time, Pallas kernels for 0%

profile of v1, /device:TPU:0, one launch (start us, length us, event | category | flops | bytes accessed | tf_op | source)
XLA Modules:
  0.0 364.5 jit_solution(6873388799679377124)
XLA Ops:
  8.7 36.6 %all-gather.14.cloned.1.call-done = bf16[1,2048,512]{2,1,0:T(8,128)(2,1)} async-done(((bf16[1,2048,256]{2,1,0:T(8,128)(2,1)}), bf16[1,2048,512]{2,1,0:T(8,128)(2,1)}) %all-gather.14.cloned.1.call-update) | async-done | bytes 2097168 | tf_op jit(solution)/shard_map/all_gather | solution.py:35
  45.4 2.9 fusion.27
  55.1 25.0 %all-gather.12.cloned.1.call-done = bf16[1,512,2048]{2,1,0:T(8,128)(2,1)} async-done(((bf16[1,256,2048]{2,1,0:T(8,128)(2,1)}), bf16[1,512,2048]{2,1,0:T(8,128)(2,1)}) %all-gather.12.cloned.1.call-update) | async-done | bytes 2097168 | tf_op jit(solution)/shard_map/all_gather | solution.py:36
  80.1 2.4 fusion.41
  82.5 7.6 %all-gather.1 = f32[256,512]{1,0:T(8,128)} all-gather(f32[64,512]{1,0:T(8,128)S(1)} %fusion.41), channel_id=3, replica_groups=mesh['pipe'=4,'dp'=2,'tensor'=4] {'tensor'}, dimensions={0}, use_global_device_ids=true | all-gather | bytes 655360 | tf_op jit(solution)/shard_map/all_gather | solution.py:8
  91.2 28.3 %all-reduce.3.cloned.1.call-done = (f32[64,512]{1,0:T(8,128)}, f32[64,512]{1,0:T(8,128)}, f32[64,512]{1,0:T(8,128)}, f32[64,512]{1,0:T(8,128)}, f32[64,512]{1,0:...) async-done(((f32[64,512]{1,0:T(8,128)}, f32[64,512]{1,0:T(8,128)}, f32[64,512]{1,0:T(8,128)}, f32[64,512]{1,0:T(8,128)}, f32[64,512]{1,0:T(8,128)}, ...) | async-done | bytes 917520 | tf_op jit(solution)/shard_map/psum | solution.py:54
  121.6 2.5 bitcast_dynamic-update-slice_fusion
  129.1 4.6 %collective-permute-done = bf16[64,2048]{1,0:T(8,128)(2,1)} collective-permute-done((bf16[64,2048]{1,0:T(8,128)(2,1)}, bf16[64,2048]{1,0:T(8,128)(2,1)}, u32[]{:S(2)}, u32[]{:S(2)}) %collective-permute-start) | collective-permute-done | bytes 262176 | tf_op jit(solution)/shard_map/ppermute | solution.py:14
  136.3 2.3 fusion.39
  138.6 7.6 %all-gather.3 = f32[256,512]{1,0:T(8,128)} all-gather(f32[64,512]{1,0:T(8,128)S(1)} %fusion.39), channel_id=5, replica_groups=mesh['pipe'=4,'dp'=2,'tensor'=4] {'tensor'}, dimensions={0}, use_global_device_ids=true | all-gather | bytes 655360 | tf_op jit(solution)/shard_map/all_gather | solution.py:8
  148.9 2.6 fusion.62
  152.8 9.5 %collective-permute-done.1 = bf16[64,2048]{1,0:T(8,128)(2,1)} collective-permute-done((bf16[64,2048]{1,0:T(8,128)(2,1)}, bf16[64,2048]{1,0:T(8,128)(2,1)}, u32[]{:S(2)}, u32[]{:S(2)}) %collective-permute-start.1) | collective-permute-done | bytes 262176 | tf_op jit(solution)/shard_map/ppermute | solution.py:14
  167.2 7.0 %all-gather.4 = f32[256,512]{1,0:T(8,128)} all-gather(f32[64,512]{1,0:T(8,128)S(1)} %fusion.37), channel_id=6, replica_groups=mesh['pipe'=4,'dp'=2,'tensor'=4] {'tensor'}, dimensions={0}, use_global_device_ids=true | all-gather | bytes 655360 | tf_op jit(solution)/shard_map/all_gather | solution.py:8
  176.9 2.6 fusion.60
  180.7 9.5 %collective-permute-done.2 = bf16[64,2048]{1,0:T(8,128)(2,1)} collective-permute-done((bf16[64,2048]{1,0:T(8,128)(2,1)}, bf16[64,2048]{1,0:T(8,128)(2,1)}, u32[]{:S(2)}, u32[]{:S(2)}) %collective-permute-start.2) | collective-permute-done | bytes 262176 | tf_op jit(solution)/shard_map/ppermute | solution.py:14
  192.8 2.3 fusion.35
  195.2 7.3 %all-gather.5 = f32[256,512]{1,0:T(8,128)} all-gather(f32[64,512]{1,0:T(8,128)S(1)} %fusion.35), channel_id=7, replica_groups=mesh['pipe'=4,'dp'=2,'tensor'=4] {'tensor'}, dimensions={0}, use_global_device_ids=true | all-gather | bytes 655360 | tf_op jit(solution)/shard_map/all_gather | solution.py:8
  205.2 2.6 fusion.58
  209.1 9.5 %collective-permute-done.3 = bf16[64,2048]{1,0:T(8,128)(2,1)} collective-permute-done((bf16[64,2048]{1,0:T(8,128)(2,1)}, bf16[64,2048]{1,0:T(8,128)(2,1)}, u32[]{:S(2)}, u32[]{:S(2)}) %collective-permute-start.3) | collective-permute-done | bytes 262176 | tf_op jit(solution)/shard_map/ppermute | solution.py:14
  221.2 2.3 fusion.33
  223.5 7.0 %all-gather.6 = f32[256,512]{1,0:T(8,128)} all-gather(f32[64,512]{1,0:T(8,128)S(1)} %fusion.33), channel_id=8, replica_groups=mesh['pipe'=4,'dp'=2,'tensor'=4] {'tensor'}, dimensions={0}, use_global_device_ids=true | all-gather | bytes 655360 | tf_op jit(solution)/shard_map/all_gather | solution.py:8
  233.2 2.6 fusion.56
  237.0 9.5 %collective-permute-done.4 = bf16[64,2048]{1,0:T(8,128)(2,1)} collective-permute-done((bf16[64,2048]{1,0:T(8,128)(2,1)}, bf16[64,2048]{1,0:T(8,128)(2,1)}, u32[]{:S(2)}, u32[]{:S(2)}) %collective-permute-start.4) | collective-permute-done | bytes 262176 | tf_op jit(solution)/shard_map/ppermute | solution.py:14
  251.5 7.3 %all-gather.7 = f32[256,512]{1,0:T(8,128)} all-gather(f32[64,512]{1,0:T(8,128)S(1)} %fusion.31), channel_id=9, replica_groups=mesh['pipe'=4,'dp'=2,'tensor'=4] {'tensor'}, dimensions={0}, use_global_device_ids=true | all-gather | bytes 655360 | tf_op jit(solution)/shard_map/all_gather | solution.py:8
  261.5 2.6 fusion.54
  265.6 9.3 %collective-permute-done.5 = bf16[64,2048]{1,0:T(8,128)(2,1)} collective-permute-done((bf16[64,2048]{1,0:T(8,128)(2,1)}, bf16[64,2048]{1,0:T(8,128)(2,1)}, u32[]{:S(2)}, u32[]{:S(2)}) %collective-permute-start.5) | collective-permute-done | bytes 262176 | tf_op jit(solution)/shard_map/ppermute | solution.py:14
  279.8 7.0 %all-gather.8 = f32[256,512]{1,0:T(8,128)} all-gather(f32[64,512]{1,0:T(8,128)S(1)} %fusion.29), channel_id=10, replica_groups=mesh['pipe'=4,'dp'=2,'tensor'=4] {'tensor'}, dimensions={0}, use_global_device_ids=true | all-gather | bytes 655360 | tf_op jit(solution)/shard_map/all_gather | solution.py:8
  292.5 3.3 bitcast_convert_fusion
  295.8 2.3 copy.42
  298.2 2.4 fusion.46
  300.6 22.7 %reduce-scatter.3.cloned.1.call-done = bf16[2048,256]{0,1:T(8,128)(2,1)} async-done(((bf16[2048,512]{0,1:T(8,128)(2,1)}), bf16[2048,256]{0,1:T(8,128)(2,1)}) %reduce-scatter.3.cloned.1.call-update) | async-done | bytes 1048592 | tf_op jit(solution)/shard_map/reduce_scatter | solution.py:83
  325.6 32.4 %reduce-scatter.5.cloned.1.call-done = bf16[256,2048]{1,0:T(8,128)(2,1)} async-done(((bf16[512,2048]{1,0:T(8,128)(2,1)}), bf16[256,2048]{1,0:T(8,128)(2,1)}) %reduce-scatter.5.cloned.1.call-update) | async-done | bytes 1048592 | tf_op jit(solution)/shard_map/reduce_scatter | solution.py:86
  (79 shorter events, 67.2 us)
Async XLA Ops:
  7.2 38.2 %copy-start = (bf16[1,4,64,2048]{3,2,1,0:T(8,128)(2,1)S(1)}, bf16[1,4,64,2048]{3,2,1,0:T(8,128)(2,1)}, u32[]{:S(2)}) copy-start(bf16[1,4,64,2048]{3,2,1,0:T(8,128)(2,1)} %param.4) | copy-start | bytes 3145732
  7.2 38.2 %all-gather.14.cloned.1.call-start = ((), (), s32[]{:S(2)}) async-start(), calls=%async_computation.5 | async-start | bytes 3145728 | tf_op jit(solution)/shard_map/all_gather | solution.py:35
  7.9 72.1 %all-gather.12.cloned.1.call-start = ((), (), s32[]{:S(2)}) async-start(), calls=%async_computation.4 | async-start | bytes 3145728 | tf_op jit(solution)/shard_map/all_gather | solution.py:36
  8.7 110.9 %all-reduce.3.cloned.1.call-start = ((), (), s32[]{:S(2)}) async-start(), calls=%async_computation.6 | async-start | bytes 1835008 | tf_op jit(solution)/shard_map/psum | solution.py:54
  45.4 2.9 copy-start.1
  55.0 268.3 %reduce-scatter.3.cloned.1.call-start = ((), (), s32[]{:S(2)}) async-start(), calls=%async_computation.2 | async-start | bytes 3145728 | tf_op jit(solution)/shard_map/reduce_scatter | solution.py:83
  121.6 6.7 %copy-start.11 = (f32[64,512]{1,0:T(8,128)S(1)}, f32[64,512]{1,0:T(8,128)}, u32[]{:S(2)}) copy-start(f32[64,512]{1,0:T(8,128)} %get-tuple-element.6) | copy-start | bytes 393220
  124.1 9.5 %collective-permute-start = (bf16[64,2048]{1,0:T(8,128)(2,1)}, bf16[64,2048]{1,0:T(8,128)(2,1)}, u32[]{:S(2)}, u32[]{:S(2)}) collective-permute-start(bf16[64,2048]{1,0:T(8,128)(2,1)} %get-tuple-element.56), channel_id=1, source_target_pairs={{8,0},{16,8},{24,16},{9,1},{17,9},{25,17},{10,2},{18,10},{26,18},{... | collective-permute-start | bytes 786440 | tf_op jit(solution)/shard_map/ppermute | solution.py:14
  128.3 0.7 copy-start.9
  135.6 0.7 copy-start.2
  151.5 10.8 %collective-permute-start.1 = (bf16[64,2048]{1,0:T(8,128)(2,1)}, bf16[64,2048]{1,0:T(8,128)(2,1)}, u32[]{:S(2)}, u32[]{:S(2)}) collective-permute-start(bf16[64,2048]{1,0:T(8,128)(2,1)} %get-tuple-element.48), channel_id=1, source_target_pairs={{8,0},{16,8},{24,16},{9,1},{17,9},{25,17},{10,2},{18,10},{26,18},{... | collective-permute-start | bytes 786440 | tf_op jit(solution)/shard_map/ppermute | solution.py:14
  164.2 0.7 copy-start.3
  179.5 10.8 %collective-permute-start.2 = (bf16[64,2048]{1,0:T(8,128)(2,1)}, bf16[64,2048]{1,0:T(8,128)(2,1)}, u32[]{:S(2)}, u32[]{:S(2)}) collective-permute-start(bf16[64,2048]{1,0:T(8,128)(2,1)} %get-tuple-element.46), channel_id=1, source_target_pairs={{8,0},{16,8},{24,16},{9,1},{17,9},{25,17},{10,2},{18,10},{26,18},{... | collective-permute-start | bytes 786440 | tf_op jit(solution)/shard_map/ppermute | solution.py:14
  192.1 0.7 copy-start.4
  207.8 10.8 %collective-permute-start.3 = (bf16[64,2048]{1,0:T(8,128)(2,1)}, bf16[64,2048]{1,0:T(8,128)(2,1)}, u32[]{:S(2)}, u32[]{:S(2)}) collective-permute-start(bf16[64,2048]{1,0:T(8,128)(2,1)} %get-tuple-element.44), channel_id=1, source_target_pairs={{8,0},{16,8},{24,16},{9,1},{17,9},{25,17},{10,2},{18,10},{26,18},{... | collective-permute-start | bytes 786440 | tf_op jit(solution)/shard_map/ppermute | solution.py:14
  220.5 0.7 copy-start.5
  235.8 10.8 %collective-permute-start.4 = (bf16[64,2048]{1,0:T(8,128)(2,1)}, bf16[64,2048]{1,0:T(8,128)(2,1)}, u32[]{:S(2)}, u32[]{:S(2)}) collective-permute-start(bf16[64,2048]{1,0:T(8,128)(2,1)} %get-tuple-element.42), channel_id=1, source_target_pairs={{8,0},{16,8},{24,16},{9,1},{17,9},{25,17},{10,2},{18,10},{26,18},{... | collective-permute-start | bytes 786440 | tf_op jit(solution)/shard_map/ppermute | solution.py:14
  248.4 0.7 copy-start.6
  264.1 10.8 %collective-permute-start.5 = (bf16[64,2048]{1,0:T(8,128)(2,1)}, bf16[64,2048]{1,0:T(8,128)(2,1)}, u32[]{:S(2)}, u32[]{:S(2)}) collective-permute-start(bf16[64,2048]{1,0:T(8,128)(2,1)} %get-tuple-element.40), channel_id=1, source_target_pairs={{8,0},{16,8},{24,16},{9,1},{17,9},{25,17},{10,2},{18,10},{26,18},{... | collective-permute-start | bytes 786440 | tf_op jit(solution)/shard_map/ppermute | solution.py:14
  276.8 0.7 copy-start.7
  291.6 0.9 copy-start.10
  291.6 66.3 %reduce-scatter.5.cloned.1.call-start = ((), (), s32[]{:S(2)}) async-start(), calls=%async_computation.3 | async-start | bytes 3145728 | tf_op jit(solution)/shard_map/reduce_scatter | solution.py:86
  295.8 2.4 copy-start.8
  295.8 2.4 copy-start.12
Sparse Core Ops, SparseCore 0:
  9.5 35.7 all-gather.13
  46.9 33.1 all-gather.11
  83.5 35.9 all-reduce.2
  291.7 31.5 reduce-scatter.2
  326.1 31.8 reduce-scatter.4
